TPU v7x, 32 devices: a whole 2x2x4 slice. The times are simulated.
32 devices in a mesh: dp: 2 (over y), expert: 16 (over z, x, core).
Axes of the slice: x: 2, y: 2, z: 4, core: 2. Of those that a mesh axis runs over, the one named last changes fastest.
Arguments:
- tokens: bfloat16 [32768, 768], P(('dp', 'expert')), may hold values from -6 to 6
- routes: int32 [32768, 1], P(('dp', 'expert')), may hold values from 0 to 15
- cotangent: bfloat16 [32768, 768], P(('dp', 'expert')), may hold values from -6 to 6
- gain_first: bfloat16 [768], replicated, may hold values from 0.5 to 1.5
- w_query: bfloat16 [768, 768], replicated, may hold values from -0.21875 to 0.21875
- w_key: bfloat16 [768, 768], replicated, may hold values from -0.21875 to 0.21875
- w_value: bfloat16 [768, 768], replicated, may hold values from -0.21875 to 0.21875
- w_output: bfloat16 [768, 768], replicated, may hold values from -1.75 to 1.75
- bias_table: bfloat16 [32, 12], replicated, may hold values from -4 to 4
- gain_second: bfloat16 [768], replicated, may hold values from 0.5 to 1.5
- w_router: bfloat16 [768, 16], replicated, may hold values from -0.109375 to 0.109375
- expert_in: bfloat16 [16, 768, 3072], P('expert'), may hold values from -0.21875 to 0.21875
- expert_out: bfloat16 [16, 3072, 768], P('expert'), may hold values from -2.5 to 2.5
Outputs:
- out_tokens: bfloat16 [32768, 768], P(('dp', 'expert'))
- grad_tokens: float32 [32768, 768], P(('dp', 'expert'))
- grad_gain_first: float32 [768], replicated
- grad_query: float32 [768, 768], replicated
- grad_key: float32 [768, 768], replicated
- grad_value: float32 [768, 768], replicated
- grad_output: float32 [768, 768], replicated
- grad_table: float32 [32, 12], replicated
- grad_gain_second: float32 [768], replicated
- grad_router: float32 [768, 16], replicated
- grad_expert_in: float32 [16, 768, 3072], P('expert', None, 'dp')
- grad_expert_out: float32 [16, 3072, 768], P('expert', 'dp')
All inputs are finite; a program needn't handle non-finite values.
Results may differ from a plain program's by a relative error of at most 0.015.
Values may be sent and summed in bfloat16 or wider, within the bound.
A program may use at most 320 MiB of HBM per device.

v0:
```python
import jax
import jax.numpy as jnp
from jax import lax
from jax.sharding import PartitionSpec as P

eps_norm = 1e-06
thresholds = (12, 16, 23, 32, 46, 64, 91)


def relative_buckets(query_pos, key_pos):
    offset = key_pos[None, :] - query_pos[:, None]
    distance = jnp.abs(offset)
    far_bucket = 8 + sum(((distance >= threshold).astype(jnp.int32) for threshold in thresholds))
    near_far = jnp.where(distance < 8, distance, far_bucket)
    return near_far + 16 * (offset > 0).astype(jnp.int32)


def rms_norm(values, gain_vector):
    scale = lax.rsqrt(jnp.mean(values * values, axis=-1, keepdims=True) + eps_norm)
    return values * scale * gain_vector


def score_block(query_rows, key_low, bias_table, row_start, scale):
    block_rows = query_rows.shape[0]
    query_pos = row_start + jnp.arange(block_rows, dtype=jnp.int32)
    key_pos = jnp.arange(key_low.shape[0], dtype=jnp.int32)
    buckets = relative_buckets(query_pos, key_pos)
    onehot = (
        buckets[:, :, None] == jnp.arange(bias_table.shape[0], dtype=jnp.int32)[None, None, :]
    ).astype(jnp.bfloat16)
    scores = (
        jnp.einsum("qhd,khd->hqk", query_rows, key_low, preferred_element_type=jnp.float32) * scale
    )
    scores = scores + jnp.einsum(
        "qkb,bh->hqk", onehot, bias_table, preferred_element_type=jnp.float32
    )
    return (scores, onehot)


def local(
    tokens,
    routes,
    cotangent,
    gain_first,
    w_query,
    w_key,
    w_value,
    w_output,
    bias_table,
    gain_second,
    w_router,
    expert_in,
    expert_out,
):
    seq_len, model_width = tokens.shape
    head_count = bias_table.shape[1]
    head_size = model_width // head_count
    experts_all = w_router.shape[1]
    capacity = (5 * seq_len + 4 * experts_all - 1) // (4 * experts_all)
    scale = head_size ** (-0.5)
    block_rows = min(512, seq_len)
    block_count = seq_len // block_rows
    inputs = tokens.astype(jnp.float32)
    normed_one, norm_one_back = jax.vjp(rms_norm, inputs, gain_first.astype(jnp.float32))
    normed_low = normed_one.astype(jnp.bfloat16)
    query_low = (
        jnp.dot(normed_low, w_query, preferred_element_type=jnp.float32)
        .astype(jnp.bfloat16)
        .reshape(seq_len, head_count, head_size)
    )
    key_low = (
        jnp.dot(normed_low, w_key, preferred_element_type=jnp.float32)
        .astype(jnp.bfloat16)
        .reshape(seq_len, head_count, head_size)
    )
    value_low = (
        jnp.dot(normed_low, w_value, preferred_element_type=jnp.float32)
        .astype(jnp.bfloat16)
        .reshape(seq_len, head_count, head_size)
    )
    mixed_parts = []
    lse_parts = []
    for block_index in range(block_count):
        row_start = block_index * block_rows
        query_rows = query_low[row_start : row_start + block_rows]
        scores, onehot = score_block(query_rows, key_low, bias_table, row_start, scale)
        row_max = jnp.max(scores, axis=-1, keepdims=True)
        exp_scores = jnp.exp(scores - row_max)
        row_total = jnp.sum(exp_scores, axis=-1, keepdims=True)
        attn_probs = exp_scores / row_total
        lse_parts.append(row_max + jnp.log(row_total))
        mixed_parts.append(
            jnp.einsum(
                "hqk,khd->qhd",
                attn_probs.astype(jnp.bfloat16),
                value_low,
                preferred_element_type=jnp.float32,
            )
        )
    attn_low = (
        jnp.concatenate(mixed_parts, axis=0).reshape(seq_len, model_width).astype(jnp.bfloat16)
    )
    after_attn = inputs + jnp.dot(attn_low, w_output, preferred_element_type=jnp.float32)
    normed_two, norm_two_back = jax.vjp(rms_norm, after_attn, gain_second.astype(jnp.float32))
    routed_low = normed_two.astype(jnp.bfloat16)
    logits = jnp.dot(routed_low, w_router, preferred_element_type=jnp.float32)
    router_probs = jax.nn.softmax(logits, axis=-1)
    choice_ids = routes[:, 0]
    expert_hot = (choice_ids[:, None] == jnp.arange(experts_all, dtype=jnp.int32)[None, :]).astype(
        jnp.int32
    )
    position = jnp.sum(jnp.cumsum(expert_hot, axis=0) * expert_hot, axis=1) - 1
    slot_hot = position[:, None] == jnp.arange(capacity, dtype=jnp.int32)[None, :]
    dispatch_table = (
        ((expert_hot[:, :, None] > 0) & slot_hot[:, None, :])
        .astype(jnp.bfloat16)
        .reshape(seq_len, experts_all * capacity)
    )
    hot_float = expert_hot.astype(jnp.float32)
    gate_value = jnp.sum(router_probs * hot_float, axis=1)
    slot_rows = jnp.einsum(
        "ts,td->sd", dispatch_table, routed_low, preferred_element_type=jnp.float32
    )
    slot_rows = slot_rows.astype(jnp.bfloat16).reshape(experts_all, 1, capacity, model_width)
    received = lax.all_to_all(slot_rows, "expert", split_axis=0, concat_axis=1, tiled=True)
    hidden_pre = jnp.einsum(
        "esrd,edf->esrf", received, expert_in, preferred_element_type=jnp.float32
    )
    activated = jax.nn.gelu(hidden_pre, approximate=True).astype(jnp.bfloat16)
    produced = jnp.einsum(
        "esrf,efd->esrd", activated, expert_out, preferred_element_type=jnp.float32
    ).astype(jnp.bfloat16)
    returned = lax.all_to_all(produced, "expert", split_axis=1, concat_axis=0, tiled=True)
    returned, hidden_pre, received = (returned, hidden_pre, received)
    combined = jnp.dot(
        dispatch_table,
        returned.reshape(experts_all * capacity, model_width),
        preferred_element_type=jnp.float32,
    )
    output = (after_attn + gate_value[:, None] * combined).astype(jnp.bfloat16)
    upstream = cotangent.astype(jnp.float32)
    gate_grad = jnp.sum(upstream * combined, axis=1)
    token_grad_low = (gate_value[:, None] * upstream).astype(jnp.bfloat16)
    slot_grads = jnp.einsum(
        "ts,td->sd", dispatch_table, token_grad_low, preferred_element_type=jnp.float32
    )
    slot_grads = slot_grads.astype(jnp.bfloat16).reshape(experts_all, 1, capacity, model_width)
    arrived = lax.all_to_all(slot_grads, "expert", split_axis=0, concat_axis=1, tiled=True)
    activated_full, gelu_back = jax.vjp(
        lambda pre_value: jax.nn.gelu(pre_value, approximate=True), hidden_pre
    )
    activated_low = activated_full.astype(jnp.bfloat16)
    act_grad = jnp.einsum("esrd,efd->esrf", arrived, expert_out, preferred_element_type=jnp.float32)
    pre_grad_low = gelu_back(act_grad)[0].astype(jnp.bfloat16)
    input_grad_low = jnp.einsum(
        "esrf,edf->esrd", pre_grad_low, expert_in, preferred_element_type=jnp.float32
    ).astype(jnp.bfloat16)
    sent_back = lax.all_to_all(input_grad_low, "expert", split_axis=1, concat_axis=0, tiled=True)
    full_in = jnp.einsum(
        "esrd,esrf->edf", received, pre_grad_low, preferred_element_type=jnp.float32
    )
    full_out = jnp.einsum(
        "esrf,esrd->efd", activated_low, arrived, preferred_element_type=jnp.float32
    )
    grad_in, grad_out = (
        lax.psum_scatter(
            full_in.astype(jnp.bfloat16), "dp", scatter_dimension=2, tiled=True
        ).astype(jnp.float32),
        lax.psum_scatter(
            full_out.astype(jnp.bfloat16), "dp", scatter_dimension=1, tiled=True
        ).astype(jnp.float32),
    )
    logit_grad_low = ((gate_grad * gate_value)[:, None] * (hot_float - router_probs)).astype(
        jnp.bfloat16
    )
    grad_router = jnp.einsum(
        "td,te->de", routed_low, logit_grad_low, preferred_element_type=jnp.float32
    )
    routed_grad = jnp.dot(
        dispatch_table,
        sent_back.reshape(experts_all * capacity, model_width),
        preferred_element_type=jnp.float32,
    )
    routed_grad = routed_grad + jnp.einsum(
        "te,de->td", logit_grad_low, w_router, preferred_element_type=jnp.float32
    )
    resid_grad, gain_two_grad = norm_two_back(routed_grad)
    after_grad = upstream + resid_grad
    branch_low = after_grad.astype(jnp.bfloat16)
    grad_output_w = jnp.einsum(
        "td,te->de", attn_low, branch_low, preferred_element_type=jnp.float32
    )
    attn_grad_low = jnp.einsum(
        "te,de->td", branch_low, w_output, preferred_element_type=jnp.float32
    )
    attn_grad_low = attn_grad_low.astype(jnp.bfloat16).reshape(seq_len, head_count, head_size)
    query_parts = []
    key_grad = jnp.zeros((seq_len, head_count, head_size), jnp.float32)
    value_grad = jnp.zeros((seq_len, head_count, head_size), jnp.float32)
    table_grad = jnp.zeros(bias_table.shape, jnp.float32)
    for block_index in range(block_count):
        row_start = block_index * block_rows
        query_rows = query_low[row_start : row_start + block_rows]
        scores, onehot = score_block(query_rows, key_low, bias_table, row_start, scale)
        attn_probs = jnp.exp(scores - lse_parts[block_index])
        grad_rows = attn_grad_low[row_start : row_start + block_rows]
        prob_grad = jnp.einsum(
            "qhd,khd->hqk", grad_rows, value_low, preferred_element_type=jnp.float32
        )
        row_dot = jnp.sum(attn_probs * prob_grad, axis=-1, keepdims=True)
        score_grad_low = (attn_probs * (prob_grad - row_dot)).astype(jnp.bfloat16)
        query_parts.append(
            scale
            * jnp.einsum(
                "hqk,khd->qhd", score_grad_low, key_low, preferred_element_type=jnp.float32
            )
        )
        key_grad = key_grad + scale * jnp.einsum(
            "hqk,qhd->khd", score_grad_low, query_rows, preferred_element_type=jnp.float32
        )
        value_grad = value_grad + jnp.einsum(
            "hqk,qhd->khd",
            attn_probs.astype(jnp.bfloat16),
            grad_rows,
            preferred_element_type=jnp.float32,
        )
        table_grad = table_grad + jnp.einsum(
            "qkb,hqk->bh", onehot, score_grad_low, preferred_element_type=jnp.float32
        )
    query_grad_low = (
        jnp.concatenate(query_parts, axis=0).reshape(seq_len, model_width).astype(jnp.bfloat16)
    )
    key_grad_low = key_grad.reshape(seq_len, model_width).astype(jnp.bfloat16)
    value_grad_low = value_grad.reshape(seq_len, model_width).astype(jnp.bfloat16)
    grad_query_w = jnp.einsum(
        "td,te->de", normed_low, query_grad_low, preferred_element_type=jnp.float32
    )
    grad_key_w = jnp.einsum(
        "td,te->de", normed_low, key_grad_low, preferred_element_type=jnp.float32
    )
    grad_value_w = jnp.einsum(
        "td,te->de", normed_low, value_grad_low, preferred_element_type=jnp.float32
    )
    normed_grad = jnp.einsum(
        "te,de->td", query_grad_low, w_query, preferred_element_type=jnp.float32
    )
    normed_grad = normed_grad + jnp.einsum(
        "te,de->td", key_grad_low, w_key, preferred_element_type=jnp.float32
    )
    normed_grad = normed_grad + jnp.einsum(
        "te,de->td", value_grad_low, w_value, preferred_element_type=jnp.float32
    )
    input_resid, gain_one_grad = norm_one_back(normed_grad)
    input_grad = after_grad + input_resid
    summed = lax.psum(
        (
            gain_one_grad,
            grad_query_w,
            grad_key_w,
            grad_value_w,
            grad_output_w,
            table_grad,
            gain_two_grad,
            grad_router,
        ),
        ("dp", "expert"),
    )
    return (
        output,
        input_grad,
        summed[0],
        summed[1],
        summed[2],
        summed[3],
        summed[4],
        summed[5],
        summed[6],
        summed[7],
        grad_in,
        grad_out,
    )


def solution(mesh):
    in_specs = (
        P(("dp", "expert"), None),
        P(("dp", "expert"), None),
        P(("dp", "expert"), None),
        P(),
        P(),
        P(),
        P(),
        P(),
        P(),
        P(),
        P(),
        P("expert", None, None),
        P("expert", None, None),
    )
    out_specs = (
        P(("dp", "expert"), None),
        P(("dp", "expert"), None),
        P(),
        P(),
        P(),
        P(),
        P(),
        P(),
        P(),
        P(),
        P("expert", None, "dp"),
        P("expert", "dp", None),
    )
    return jax.shard_map(local, mesh=mesh, in_specs=in_specs, out_specs=out_specs, check_vma=False)
```

profile of v0, /device:TPU:0, one launch (start us, length us, event | category | flops | bytes accessed | tf_op | source)
XLA Modules:
  0.0 826.7 jit_solution(2873751279195848415)
XLA Ops:
  36.9 16.6 %fusion.3 = f32[512,1024,12]{0,2,1:T(8,128)} fusion(s32[512,1024]{0,1:T(8,128)S(1)} %copy-done.14, bf16[32,12]{0,1:T(8,128)(2,1)S(1)} %copy-done.62), kind=kOutput, calls=%fused_computation.5 | convolution fusion | flops 419430400 | bytes 27263744 | tf_op jit(solution)/shard_map/qkb,bh->hqk/dot_general | solution.py:34
  53.5 30.4 %copy.61 = f32[512,1024,12]{1,0,2:T(8,128)} copy(f32[512,1024,12]{0,2,1:T(8,128)} %fusion.3) | data formatting | bytes 50331648 | tf_op jit(solution)/shard_map/qkb,bh->hqk/dot_general | solution.py:34
  83.9 15.6 %fusion.1 = f32[512,1024,12]{0,2,1:T(8,128)} fusion(s32[512,1024]{0,1:T(8,128)} %fusion.49, bf16[32,12]{0,1:T(8,128)(2,1)S(1)} %copy-done.62), kind=kOutput, calls=%fused_computation.2 | convolution fusion | flops 419430400 | bytes 27263744 | tf_op jit(solution)/shard_map/qkb,bh->hqk/dot_general | solution.py:34
  99.5 30.4 %copy.62 = f32[512,1024,12]{1,0,2:T(8,128)} copy(f32[512,1024,12]{0,2,1:T(8,128)} %fusion.1) | data formatting | bytes 50331648 | tf_op jit(solution)/shard_map/qkb,bh->hqk/dot_general | solution.py:34
  129.9 16.9 %fusion.121 = (f32[12,512]{1,0:T(8,128)}, f32[12,512,1024]{2,1,0:T(8,128)}) fusion(f32[512,1024,12]{1,0,2:T(8,128)} %copy.61, bf16[512,12,64]{0,2,1:T(8,128)(2,1)} %bitcast.171, bf16[1024,12,64]{0,2,1:T(8,128)(2,1)S(1)} %bitcast.165), kind=kOutput, calls=%fused_computation.173 | convolution fusion | flops 824174592 | bytes 52715520 | tf_op jit(solution)/shard_map/qhd,khd->hqk/dot_general | solution.py:32
  169.3 17.1 %fusion.120 = (f32[12,512]{1,0:T(8,128)}, f32[12,512,1024]{2,1,0:T(8,128)}) fusion(f32[512,1024,12]{1,0,2:T(8,128)} %copy.62, bf16[512,12,64]{0,2,1:T(8,128)(2,1)S(1)} %bitcast.169, bf16[1024,12,64]{0,2,1:T(8,128)(2,1)S(1)} %bitcast.166), kind=kOutput, calls=%fused_computation.172 | convolution fusion | flops 824174592 | bytes 52715520 | tf_op jit(solution)/shard_map/qhd,khd->hqk/dot_general | solution.py:32
  233.3 30.5 %all-to-all-done = bf16[16,1,80,768]{3,2,1,0:T(8,128)(2,1)} async-done(((bf16[16,1,80,768]{3,2,1,0:T(8,128)(2,1)}), bf16[16,1,80,768]{3,2,1,0:T(8,128)(2,1)}, u32[]{:S(2)}, u32[]{:S(2)}) %all-to-all-start) | async-done | bytes 1966112 | tf_op jit(solution)/shard_map/all_to_all | solution.py:125
  274.6 12.4 %fusion.33 = f32[16,80,3072]{2,1,0:T(8,128)} fusion(bf16[1,768,3072]{2,1,0:T(8,128)(2,1)} %param.24, bf16[16,1,80,768]{3,2,1,0:T(8,128)(2,1)} %all-to-all-done), kind=kOutput, calls=%fused_computation.62 | convolution fusion | flops 6039797760 | bytes 22413312 | tf_op jit(solution)/shard_map/esrd,edf->esrf/dot_general | solution.py:126
  287.0 26.3 %all-to-all-done.2 = bf16[16,1,80,768]{3,2,1,0:T(8,128)(2,1)S(1)} async-done(((bf16[16,1,80,768]{3,2,1,0:T(8,128)(2,1)}), bf16[16,1,80,768]{3,2,1,0:T(8,128)(2,1)S(1)}, u32[]{:S(2)}, u32[]{:S(2)}) %all-to-all-start.2) | async-done | bytes 1966112 | tf_op jit(solution)/shard_map/all_to_all | solution.py:148
  313.4 17.4 %fusion.18 = bf16[16,80,3072]{2,1,0:T(8,128)(2,1)S(1)} fusion(f32[16,80,3072]{2,1,0:T(8,128)} %fusion.33, bf16[1,3072,768]{2,1,0:T(8,128)(2,1)} %param.25, bf16[16,1,80,768]{3,2,1,0:T(8,128)(2,1)S(1)} %all-to-all-done.2), kind=kOutput, calls=%fused_computation.34 | convolution fusion | flops 6118440960 | bytes 30277632 | tf_op jit(solution)/shard_map/esrd,efd->esrf/dot_general | solution.py:153
  343.4 14.8 %convert_bitcast_fusion.1 = bf16[1,16,80,768]{3,2,0,1:T(8,128)(2,1)} fusion(bf16[1,3072,768]{2,1,0:T(8,128)(2,1)} %param.25, f32[16,80,3072]{2,1,0:T(8,128)} %fusion.33), kind=kOutput, calls=%fused_computation.113 | convolution fusion | flops 6076170240 | bytes 22413312 | tf_op jit(solution)/shard_map/esrf,efd->esrd/dot_general | solution.py:130
  382.1 26.3 %all-to-all-done.1 = bf16[1,16,80,768]{3,2,0,1:T(8,128)(2,1)} async-done(((bf16[1,16,80,768]{3,2,0,1:T(8,128)(2,1)}), bf16[1,16,80,768]{3,2,0,1:T(8,128)(2,1)}, u32[]{:S(2)}, u32[]{:S(2)}) %all-to-all-start.1) | async-done | bytes 1966112 | tf_op jit(solution)/shard_map/all_to_all | solution.py:133
  419.2 13.1 %fusion.38 = bf16[1,3072,768]{2,1,0:T(8,128)(2,1)} fusion(bf16[16,1,80,768]{3,2,1,0:T(8,128)(2,1)S(1)} %all-to-all-done.2, f32[16,80,3072]{2,1,0:T(8,128)} %fusion.33), kind=kOutput, calls=%fused_computation.65 | convolution fusion | flops 6077546496 | bytes 22413312 | tf_op jit(solution)/shard_map/esrf,esrd->efd/dot_general | solution.py:162
  439.6 18.4 %all-to-all-done.3 = bf16[1,16,80,768]{3,2,0,1:T(8,128)(2,1)} async-done(((bf16[1,16,80,768]{3,2,0,1:T(8,128)(2,1)}), bf16[1,16,80,768]{3,2,0,1:T(8,128)(2,1)}, u32[]{:S(2)}, u32[]{:S(2)}) %all-to-all-start.3) | async-done | bytes 1966112 | tf_op jit(solution)/shard_map/all_to_all | solution.py:158
  469.1 18.4 %multiply_reduce_fusion.1 = (f32[12,512]{1,0:T(8,128)S(1)}, f32[12,512,1024]{2,1,0:T(8,128)}) fusion(f32[12,512,1024]{2,1,0:T(8,128)} %get-tuple-element.69, f32[12,512]{1,0:T(8,128)S(1)} %copy-done.36, bf16[512,12,64]{0,2,1:T(8,128)(2,1)S(1)} %bitcast.173, bf16[1024,12,64]{0,2,1:T(8,128)(2,1)} %bitcast.177), kind=kOutput, calls=%fused_computation.16 | convolution fusion | flops 824174592 | bytes 52740096 | tf_op jit(solution)/shard_map/qhd,khd->hqk/dot_general | solution.py:207
  487.5 21.5 %multiply_convert_fusion.1 = bf16[12,512,1024]{2,1,0:T(8,128)(2,1)} fusion(f32[12,512,1024]{2,1,0:T(8,128)} %get-tuple-element.80, f32[12,512,1024]{2,1,0:T(8,128)} %get-tuple-element.69, f32[12,512]{1,0:T(8,128)S(1)} %get-tuple-element.79, f32[12,512]{1,0:T(8,128)S(1)} %copy-done.36), kind=kLoop, calls=%fused_computation.15 | loop fusion | flops 25165824 | bytes 62963712 | tf_op jit(solution)/shard_map/convert_element_type | solution.py:211
  509.0 18.9 %multiply_reduce_fusion = (f32[12,512]{1,0:T(8,128)}, f32[12,512,1024]{2,1,0:T(8,128)}) fusion(f32[12,512,1024]{2,1,0:T(8,128)} %get-tuple-element.67, f32[12,512]{1,0:T(8,128)} %log_add_fusion, bf16[512,12,64]{0,2,1:T(8,128)(2,1)S(1)} %bitcast.175, bf16[1024,12,64]{0,2,1:T(8,128)(2,1)} %bitcast.178), kind=kOutput, calls=%fused_computation.13 | convolution fusion | flops 824174592 | bytes 52740096 | tf_op jit(solution)/shard_map/qhd,khd->hqk/dot_general | solution.py:207
  536.4 21.5 %multiply_convert_fusion = bf16[12,512,1024]{2,1,0:T(8,128)(2,1)} fusion(f32[12,512,1024]{2,1,0:T(8,128)} %get-tuple-element.78, f32[12,512,1024]{2,1,0:T(8,128)} %get-tuple-element.67, f32[12,512]{1,0:T(8,128)S(1)} %copy-done.44, f32[12,512]{1,0:T(8,128)S(1)} %copy-done.37), kind=kLoop, calls=%fused_computation.12 | loop fusion | flops 25165824 | bytes 62963712 | tf_op jit(solution)/shard_map/convert_element_type | solution.py:211
  616.0 23.3 %copy.75 = bf16[12,512,1024]{1,0,2:T(8,128)(2,1)} copy(bf16[12,512,1024]{2,1,0:T(8,128)(2,1)} %multiply_convert_fusion.1) | data formatting | bytes 25165824 | tf_op jit(solution)/shard_map/convert_element_type | solution.py:211
  639.3 23.2 %copy.76 = bf16[12,512,1024]{1,0,2:T(8,128)(2,1)} copy(bf16[12,512,1024]{2,1,0:T(8,128)(2,1)} %multiply_convert_fusion) | data formatting | bytes 25165824 | tf_op jit(solution)/shard_map/convert_element_type | solution.py:211
  677.5 13.1 %fusion.86 = f32[32,12]{0,1:T(8,128)S(1)} fusion(bf16[12,512,1024]{1,0,2:T(8,128)(2,1)} %copy.75, s32[512,1024]{0,1:T(8,128)} %fusion.48), kind=kOutput, calls=%fused_computation.130 | convolution fusion | flops 419430400 | bytes 14681600 | tf_op jit(solution)/shard_map/qkb,hqk->bh/dot_general | solution.py:227
  690.6 13.4 %fusion.88 = f32[32,12]{0,1:T(8,128)S(1)} fusion(f32[32,12]{0,1:T(8,128)S(1)} %fusion.86, bf16[12,512,1024]{1,0,2:T(8,128)(2,1)} %copy.76, s32[512,1024]{0,1:T(8,128)S(1)} %copy-done.15), kind=kOutput, calls=%fused_computation.132 | convolution fusion | flops 419430784 | bytes 14683136 | tf_op jit(solution)/shard_map/qkb,hqk->bh/dot_general | solution.py:227
  704.1 48.0 %all-reduce = (f32[768]{0:T(1024)}, f32[32,12]{0,1:T(8,128)}, f32[768]{0:T(1024)}, f32[768,16]{0,1:T(8,128)}) all-reduce(f32[768]{0:T(1024)S(1)} %get-tuple-element.50, f32[32,12]{0,1:T(8,128)S(1)} %fusion.88, f32[768]{0:T(1024)S(1)} %copy-done.63, f32[768,16]{0,1:T(8,128)S(1)} %fusion.106), channel_id=1, replica_groups=mesh['dp'=2,'expert'=16] {'dp','expert'}, use_global_device_ids=true, to_apply=%region_18.19 | all-reduce | flops 14208 | bytes 113664 | tf_op jit(solution)/shard_map/psum | solution.py:255
  761.0 48.2 %all-reduce.4.cloned.1.call-done = (f32[768,768]{1,0:T(8,128)}, f32[768,768]{1,0:T(8,128)}, f32[768,768]{1,0:T(8,128)}, f32[768,768]{1,0:T(8,128)}) async-done(((f32[768,768]{1,0:T(8,128)}, f32[768,768]{1,0:T(8,128)}, f32[768,768]{1,0:T(8,128)}, f32[768,768]{1,0:T(8,128)}), (f32[768,768]{1,0:T(8,128)}, f32[768,768]{1,0:T(8,128)}, f32[768,768]{1,0:T(8,128)}, ...) | async-done | bytes 9437200 | tf_op jit(solution)/shard_map/psum | solution.py:255
  (238 shorter events, 274.3 us)
Async XLA Ops:
  8.0 22.7 %copy-start = (bf16[768,768]{1,0:T(8,128)(2,1)S(1)}, bf16[768,768]{1,0:T(8,128)(2,1)}, u32[]{:S(2)}) copy-start(bf16[768,768]{1,0:T(8,128)(2,1)} %param.19) | copy-start | bytes 3538948
  10.7 20.0 %copy-start.54 = (f32[768]{0:T(1024)}, f32[768]{0:T(1024)S(1)}, u32[]{:S(2)}) copy-start(f32[768]{0:T(1024)S(1)} %convert_element_type.295) | copy-start | bytes 9220
  27.4 141.8 %copy-start.16 = (bf16[512,768]{0,1:T(8,128)(2,1)}, bf16[512,768]{0,1:T(8,128)(2,1)S(1)}, u32[]{:S(2)}) copy-start(bf16[512,768]{0,1:T(8,128)(2,1)S(1)} %get-tuple-element.65) | copy-start | bytes 2359300
  30.7 138.5 %copy-start.3 = (bf16[1024,768]{0,1:T(8,128)(2,1)}, bf16[1024,768]{0,1:T(8,128)(2,1)S(1)}, u32[]{:S(2)}) copy-start(bf16[1024,768]{0,1:T(8,128)(2,1)S(1)} %convolution_convert_fusion.3) | copy-start | bytes 4718596
  213.9 13.7 %copy-start.9 = (bf16[1024,768]{0,1:T(8,128)(2,1)}, bf16[1024,768]{0,1:T(8,128)(2,1)S(1)}, u32[]{:S(2)}) copy-start(bf16[1024,768]{0,1:T(8,128)(2,1)S(1)} %multiply_convert_fusion.4) | copy-start | bytes 4718596
  217.4 46.4 %all-to-all-start = ((bf16[16,1,80,768]{3,2,1,0:T(8,128)(2,1)}), bf16[16,1,80,768]{3,2,1,0:T(8,128)(2,1)}, u32[]{:S(2)}, u32[]{:S(2)}) async-start(bf16[16,1,80,768]{3,2,1,0:T(8,128)(2,1)} %bitcast.185), calls=%async_computation | async-start | bytes 3932160 | tf_op jit(solution)/shard_map/all_to_all | solution.py:125
  227.9 234.5 %copy-start.29 = (f32[1024,16]{0,1:T(8,128)}, f32[1024,16]{0,1:T(8,128)S(1)}, u32[]{:S(2)}) copy-start(f32[1024,16]{0,1:T(8,128)S(1)} %get-tuple-element.73) | copy-start | bytes 196612
  227.9 234.5 %copy-start.47 = (f32[1024]{0:T(1024)}, f32[1024]{0:T(1024)S(1)}, u32[]{:S(2)}) copy-start(f32[1024]{0:T(1024)S(1)} %get-tuple-element.72) | copy-start | bytes 12292
  228.0 234.5 %copy-start.52 = (f32[1024]{0:T(1024)}, f32[1024]{0:T(1024)S(1)}, u32[]{:S(2)}) copy-start(f32[1024]{0:T(1024)S(1)} %fusion.101) | copy-start | bytes 12292
  263.8 49.5 %all-to-all-start.2 = ((bf16[16,1,80,768]{3,2,1,0:T(8,128)(2,1)}), bf16[16,1,80,768]{3,2,1,0:T(8,128)(2,1)S(1)}, u32[]{:S(2)}, u32[]{:S(2)}) async-start(bf16[16,1,80,768]{3,2,1,0:T(8,128)(2,1)} %bitcast.186), calls=%async_computation.2 | async-start | bytes 3932160 | tf_op jit(solution)/shard_map/all_to_all | solution.py:148
  274.5 477.6 %reduce-scatter.3.cloned.1.call-start = ((), (), s32[]{:S(2)}) async-start(), calls=%async_computation.6 | async-start | bytes 7077888 | tf_op jit(solution)/shard_map/reduce_scatter | solution.py:166
  358.2 50.2 %all-to-all-start.1 = ((bf16[1,16,80,768]{3,2,0,1:T(8,128)(2,1)}), bf16[1,16,80,768]{3,2,0,1:T(8,128)(2,1)}, u32[]{:S(2)}, u32[]{:S(2)}) async-start(bf16[1,16,80,768]{3,2,0,1:T(8,128)(2,1)} %convert_bitcast_fusion.1), calls=%async_computation.1 | async-start | bytes 3932160 | tf_op jit(solution)/shard_map/all_to_all | solution.py:133
  408.4 49.6 %all-to-all-start.3 = ((bf16[1,16,80,768]{3,2,0,1:T(8,128)(2,1)}), bf16[1,16,80,768]{3,2,0,1:T(8,128)(2,1)}, u32[]{:S(2)}, u32[]{:S(2)}) async-start(bf16[1,16,80,768]{3,2,0,1:T(8,128)(2,1)} %convert_bitcast_fusion), calls=%async_computation.3 | async-start | bytes 3932160 | tf_op jit(solution)/shard_map/all_to_all | solution.py:158
  419.1 337.5 %reduce-scatter.5.cloned.1.call-start = ((), (), s32[]{:S(2)}) async-start(), calls=%async_computation.7 | async-start | bytes 7077888 | tf_op jit(solution)/shard_map/reduce_scatter | solution.py:169
  432.3 376.9 %all-reduce.4.cloned.1.call-start = ((), (), s32[]{:S(2)}) async-start(), calls=%async_computation.8 | async-start | bytes 18874368 | tf_op jit(solution)/shard_map/psum | solution.py:255
  439.6 22.8 %copy-start.60 = (f32[1024]{0:T(1024)}, f32[1024]{0:T(1024)S(1)}, u32[]{:S(2)}) copy-start(f32[1024]{0:T(1024)S(1)} %mul.288) | copy-start | bytes 12292
  468.5 19.1 %copy-start.18 = (bf16[512,768]{0,1:T(8,128)(2,1)}, bf16[512,768]{0,1:T(8,128)(2,1)S(1)}, u32[]{:S(2)}) copy-start(bf16[512,768]{0,1:T(8,128)(2,1)S(1)} %get-tuple-element.62) | copy-start | bytes 2359300
  509.0 18.9 %copy-start.4 = (bf16[1024,768]{0,1:T(8,128)(2,1)S(1)}, bf16[1024,768]{0,1:T(8,128)(2,1)}, u32[]{:S(2)}) copy-start(bf16[1024,768]{0,1:T(8,128)(2,1)} %copy-done.3) | copy-start | bytes 4718596
  578.5 12.2 %copy-start.8 = (bf16[1024,768]{0,1:T(8,128)(2,1)S(1)}, bf16[1024,768]{0,1:T(8,128)(2,1)}, u32[]{:S(2)}) copy-start(bf16[1024,768]{0,1:T(8,128)(2,1)} %copy-done.5) | copy-start | bytes 4718596
  578.5 12.2 %copy-start.55 = (f32[768]{0:T(1024)S(1)}, f32[768]{0:T(1024)}, u32[]{:S(2)}) copy-start(f32[768]{0:T(1024)} %copy-done.54) | copy-start | bytes 9220
  578.5 19.5 %slice-start.3 = ((s8[12582912]{0:T(1024)(128)(4,1)}), s8[4194304]{0:T(1024)(128)(4,1)S(1)}, s32[]{:S(2)}) async-start(s8[12582912]{0:T(1024)(128)(4,1)} %bitcast.163), calls=%async_computation.12 | async-start | bytes 8388608
  578.5 19.5 %slice-start.4 = ((s8[12582912]{0:T(1024)(128)(4,1)}), s8[4194304]{0:T(1024)(128)(4,1)S(1)}, s32[]{:S(2)}) async-start(s8[12582912]{0:T(1024)(128)(4,1)} %bitcast.163), calls=%async_computation.13 | async-start | bytes 8388608
  677.5 13.1 %copy-start.15 = (s32[512,1024]{0,1:T(8,128)S(1)}, s32[512,1024]{0,1:T(8,128)}, u32[]{:S(2)}) copy-start(s32[512,1024]{0,1:T(8,128)} %fusion.49) | copy-start | bytes 6291460
  690.6 13.5 %copy-start.63 = (f32[768]{0:T(1024)S(1)}, f32[768]{0:T(1024)}, u32[]{:S(2)}) copy-start(f32[768]{0:T(1024)} %get-tuple-element.48) | copy-start | bytes 9220
  (57 other events, 274.1 us)
Sparse Core Ops, SparseCore 0:
  343.5 66.0 reduce-scatter.2
  432.5 61.2 reduce-scatter.4
Sparse Core Ops, SparseCore 1:
  611.3 197.9 all-reduce.3
where the time goes:
time: 837 us; the launch traced here: 827 us
  matrix products  333 us (40%)
  waiting for transfers between devices  150 us (18%)
  local copies, waits for them, and re-layouts  141 us (17%)
  other arithmetic  98.4 us (12%)
  blocking collectives  48 us (6%)
  starting transfers between devices  40.5 us (5%)
  between operations  16.6 us (2%)
    dot_general x2, local copies, waits for them, and re-layouts, score_block(): jnp.einsum('qkb,bh->hqk', onehot, bias_table, preferred_element_type=jnp....  60.8 us
    psum x1, waiting for transfers between devices, local(): lax.psum((gain_one_grad, grad_query_w, grad_key_w, grad_value_w, grad_out...  48.2 us
    psum x1, blocking collectives, local(): lax.psum((gain_one_grad, grad_query_w, grad_key_w, grad_value_w, grad_out...  48 us
    convert_element_type x2, local copies, waits for them, and re-layouts, local(): score_grad_low = (attn_probs * (prob_grad - row_dot)).astype(jnp.bfloat16)  46.5 us
    convert_element_type x2, other arithmetic, local(): score_grad_low = (attn_probs * (prob_grad - row_dot)).astype(jnp.bfloat16)  43 us
    dot_general x2, matrix products, local(): jnp.einsum('qhd,khd->hqk', grad_rows, value_low, preferred_element_type=j...  37.3 us
    dot_general x2, matrix products, score_block(): jnp.einsum('qhd,khd->hqk', query_rows, key_low, preferred_element_type=jn...  34 us
    dot_general x2, matrix products, score_block(): jnp.einsum('qkb,bh->hqk', onehot, bias_table, preferred_element_type=jnp....  32.2 us
  transfers between devices with their start and end apart: 7, of which 5 were waited for; matrix products, arithmetic and copies ran while one was open for 39% of the time, Pallas kernels for 0%

commit v1 on v0

--- a/solution.py
+++ b/solution.py
@@ -252,7 +252,7 @@
     )
     input_resid, gain_one_grad = norm_one_back(normed_grad)
     input_grad = after_grad + input_resid
-    summed = lax.psum(
+    half = lax.psum(
         (
             gain_one_grad,
             grad_query_w,
@@ -263,8 +263,9 @@
             gain_two_grad,
             grad_router,
         ),
-        ("dp", "expert"),
-    )
+        "expert",
+    )
+    summed = lax.psum(half, "dp")
     return (
         output,
         input_grad,

time: 837 us -> 1020 us (1.22)
  waiting for transfers between devices: 150 us -> 302 us
  blocking collectives: 48 us -> 71.6 us
    psum x1, waiting for transfers between devices: 48.2 us -> 166 us  [local(): lax.psum((gain_one_grad, grad_query_w, grad_key_w, grad_value_w, grad_out...]
    psum x0 -> x1, waiting for transfers between devices: none -> 53.6 us  [local(): summed = lax.psum(half, 'dp')]
    all_to_all x1, waiting for transfers between devices: 26.3 us -> 8.44 us  [local(): lax.all_to_all(produced, 'expert', split_axis=1, concat_axis=0, tiled=True)]
    all_to_all x1, waiting for transfers between devices: 26.3 us -> 12.1 us  [local(): lax.all_to_all(slot_grads, 'expert', split_axis=0, concat_axis=1, tiled=T...]
    all_to_all x1, waiting for transfers between devices: 18.4 us -> 31.4 us  [local(): lax.all_to_all(input_grad_low, 'expert', split_axis=1, concat_axis=0, til...]
    psum x1, blocking collectives: 48 us -> 60.6 us  [local(): lax.psum((gain_one_grad, grad_query_w, grad_key_w, grad_value_w, grad_out...]
    psum x0 -> x1, blocking collectives: none -> 11 us  [local(): summed = lax.psum(half, 'dp')]
    unnamed x156 -> x164, local copies, waits for them, and re-layouts: 31.9 us -> 36 us
  transfers between devices with their start and end apart: 7 -> 8, of which waited for: 5 -> 6; matrix products, arithmetic and copies ran while one was open for 39% -> 18% of each run, Pallas kernels for 0% -> 0%
where the time goes in v1:
time: 1020 us; the launch traced here: 1010 us
  matrix products  335 us (33%)
  waiting for transfers between devices  302 us (30%)
  local copies, waits for them, and re-layouts  145 us (14%)
  other arithmetic  97.5 us (10%)
  blocking collectives  71.6 us (7%)
  starting transfers between devices  40.5 us (4%)
  between operations  16.7 us (2%)
    psum x1, waiting for transfers between devices, local(): lax.psum((gain_one_grad, grad_query_w, grad_key_w, grad_value_w, grad_out...  166 us
    dot_general x2, local copies, waits for them, and re-layouts, score_block(): jnp.einsum('qkb,bh->hqk', onehot, bias_table, preferred_element_type=jnp....  60.6 us
    psum x1, blocking collectives, local(): lax.psum((gain_one_grad, grad_query_w, grad_key_w, grad_value_w, grad_out...  60.6 us
    psum x1, waiting for transfers between devices, local(): summed = lax.psum(half, 'dp')  53.6 us
    convert_element_type x2, local copies, waits for them, and re-layouts, local(): score_grad_low = (attn_probs * (prob_grad - row_dot)).astype(jnp.bfloat16)  46.5 us
    convert_element_type x2, other arithmetic, local(): score_grad_low = (attn_probs * (prob_grad - row_dot)).astype(jnp.bfloat16)  43.3 us
    dot_general x2, matrix products, local(): jnp.einsum('qhd,khd->hqk', grad_rows, value_low, preferred_element_type=j...  38 us
    unnamed x164, local copies, waits for them, and re-layouts  36 us
  transfers between devices with their start and end apart: 8, of which 6 were waited for; matrix products, arithmetic and copies ran while one was open for 18% of the time, Pallas kernels for 0%

profile of v1, /device:TPU:0, one launch (start us, length us, event | category | flops | bytes accessed | tf_op | source)
XLA Modules:
  0.0 1008.4 jit_solution(2521552164683468042)
XLA Ops:
  36.9 16.3 %fusion.3 = f32[512,1024,12]{0,2,1:T(8,128)} fusion(s32[512,1024]{0,1:T(8,128)S(1)} %copy-done.15, bf16[32,12]{0,1:T(8,128)(2,1)S(1)} %copy-done.70), kind=kOutput, calls=%fused_computation.5 | convolution fusion | flops 419430400 | bytes 27263744 | tf_op jit(solution)/shard_map/qkb,bh->hqk/dot_general | solution.py:34
  53.2 30.4 %copy.61 = f32[512,1024,12]{1,0,2:T(8,128)} copy(f32[512,1024,12]{0,2,1:T(8,128)} %fusion.3) | data formatting | bytes 50331648 | tf_op jit(solution)/shard_map/qkb,bh->hqk/dot_general | solution.py:34
  83.5 15.8 %fusion.1 = f32[512,1024,12]{0,2,1:T(8,128)} fusion(s32[512,1024]{0,1:T(8,128)} %fusion.49, bf16[32,12]{0,1:T(8,128)(2,1)S(1)} %copy-done.70), kind=kOutput, calls=%fused_computation.2 | convolution fusion | flops 419430400 | bytes 27263744 | tf_op jit(solution)/shard_map/qkb,bh->hqk/dot_general | solution.py:34
  99.3 30.2 %copy.62 = f32[512,1024,12]{1,0,2:T(8,128)} copy(f32[512,1024,12]{0,2,1:T(8,128)} %fusion.1) | data formatting | bytes 50331648 | tf_op jit(solution)/shard_map/qkb,bh->hqk/dot_general | solution.py:34
  129.6 17.0 %fusion.121 = (f32[12,512]{1,0:T(8,128)}, f32[12,512,1024]{2,1,0:T(8,128)}) fusion(f32[512,1024,12]{1,0,2:T(8,128)} %copy.61, bf16[512,12,64]{0,2,1:T(8,128)(2,1)} %bitcast.167, bf16[1024,12,64]{0,2,1:T(8,128)(2,1)S(1)} %bitcast.161), kind=kOutput, calls=%fused_computation.173 | convolution fusion | flops 824174592 | bytes 52715520 | tf_op jit(solution)/shard_map/qhd,khd->hqk/dot_general | solution.py:32
  169.0 17.4 %fusion.120 = (f32[12,512]{1,0:T(8,128)}, f32[12,512,1024]{2,1,0:T(8,128)}) fusion(f32[512,1024,12]{1,0,2:T(8,128)} %copy.62, bf16[512,12,64]{0,2,1:T(8,128)(2,1)S(1)} %bitcast.165, bf16[1024,12,64]{0,2,1:T(8,128)(2,1)S(1)} %bitcast.162), kind=kOutput, calls=%fused_computation.172 | convolution fusion | flops 824174592 | bytes 52715520 | tf_op jit(solution)/shard_map/qhd,khd->hqk/dot_general | solution.py:32
  233.6 30.5 %all-to-all-done = bf16[16,1,80,768]{3,2,1,0:T(8,128)(2,1)} async-done(((bf16[16,1,80,768]{3,2,1,0:T(8,128)(2,1)}), bf16[16,1,80,768]{3,2,1,0:T(8,128)(2,1)}, u32[]{:S(2)}, u32[]{:S(2)}) %all-to-all-start) | async-done | bytes 1966112 | tf_op jit(solution)/shard_map/all_to_all | solution.py:125
  289.0 12.5 %convert_bitcast_fusion.1 = bf16[1,16,80,768]{3,2,0,1:T(8,128)(2,1)} fusion(bf16[1,3072,768]{2,1,0:T(8,128)(2,1)} %param.25, f32[16,80,3072]{2,1,0:T(8,128)S(1)} %fusion.33), kind=kOutput, calls=%fused_computation.113 | convolution fusion | flops 6076170240 | bytes 22413312 | tf_op jit(solution)/shard_map/esrf,efd->esrd/dot_general | solution.py:130
  301.6 12.1 %all-to-all-done.2 = bf16[16,1,80,768]{3,2,1,0:T(8,128)(2,1)S(1)} async-done(((bf16[16,1,80,768]{3,2,1,0:T(8,128)(2,1)}), bf16[16,1,80,768]{3,2,1,0:T(8,128)(2,1)S(1)}, u32[]{:S(2)}, u32[]{:S(2)}) %all-to-all-start.2) | async-done | bytes 1966112 | tf_op jit(solution)/shard_map/all_to_all | solution.py:148
  324.6 17.4 %fusion.18 = bf16[16,80,3072]{2,1,0:T(8,128)(2,1)S(1)} fusion(f32[16,80,3072]{2,1,0:T(8,128)} %copy-done.77, bf16[1,3072,768]{2,1,0:T(8,128)(2,1)} %param.25, bf16[16,1,80,768]{3,2,1,0:T(8,128)(2,1)S(1)} %all-to-all-done.2), kind=kOutput, calls=%fused_computation.34 | convolution fusion | flops 6118440960 | bytes 30277632 | tf_op jit(solution)/shard_map/esrd,efd->esrf/dot_general | solution.py:153
  381.7 31.4 %all-to-all-done.3 = bf16[1,16,80,768]{3,2,0,1:T(8,128)(2,1)} async-done(((bf16[1,16,80,768]{3,2,0,1:T(8,128)(2,1)}), bf16[1,16,80,768]{3,2,0,1:T(8,128)(2,1)}, u32[]{:S(2)}, u32[]{:S(2)}) %all-to-all-start.3) | async-done | bytes 1966112 | tf_op jit(solution)/shard_map/all_to_all | solution.py:158
  427.6 20.7 %multiply_reduce_fusion.1 = (f32[12,512]{1,0:T(8,128)}, f32[12,512,1024]{2,1,0:T(8,128)}) fusion(f32[12,512,1024]{2,1,0:T(8,128)} %get-tuple-element.77, f32[12,512]{1,0:T(8,128)} %log_add_fusion.1, bf16[512,12,64]{0,2,1:T(8,128)(2,1)S(1)} %bitcast.169, bf16[1024,12,64]{0,2,1:T(8,128)(2,1)S(1)} %bitcast.176), kind=kOutput, calls=%fused_computation.16 | convolution fusion | flops 824174592 | bytes 52740096 | tf_op jit(solution)/shard_map/qhd,khd->hqk/dot_general | solution.py:207
  448.3 21.7 %multiply_convert_fusion.1 = bf16[12,512,1024]{2,1,0:T(8,128)(2,1)} fusion(f32[12,512,1024]{2,1,0:T(8,128)} %get-tuple-element.88, f32[12,512,1024]{2,1,0:T(8,128)} %get-tuple-element.77, f32[12,512]{1,0:T(8,128)} %get-tuple-element.87, f32[12,512]{1,0:T(8,128)} %log_add_fusion.1), kind=kLoop, calls=%fused_computation.15 | loop fusion | flops 25165824 | bytes 62963712 | tf_op jit(solution)/shard_map/convert_element_type | solution.py:211
  488.1 12.0 %fusion.19 = f32[12,64,1024]{2,1,0:T(8,128)} fusion(bf16[512,12,64]{0,2,1:T(8,128)(2,1)S(1)} %bitcast.172, f32[12,512,1024]{2,1,0:T(8,128)} %get-tuple-element.75, f32[12,512]{1,0:T(8,128)S(1)} %copy-done.44), kind=kOutput, calls=%fused_computation.36 | convolution fusion | flops 817889280 | bytes 29122560 | tf_op jit(solution)/shard_map/hqk,qhd->khd/dot_general | solution.py:221
  500.1 17.3 %multiply_reduce_fusion = (f32[12,512]{1,0:T(8,128)}, f32[12,512,1024]{2,1,0:T(8,128)}) fusion(f32[12,512,1024]{2,1,0:T(8,128)} %get-tuple-element.75, f32[12,512]{1,0:T(8,128)} %log_add_fusion, bf16[512,12,64]{0,2,1:T(8,128)(2,1)} %bitcast.171, bf16[1024,12,64]{0,2,1:T(8,128)(2,1)} %bitcast.173), kind=kOutput, calls=%fused_computation.13 | convolution fusion | flops 824174592 | bytes 52740096 | tf_op jit(solution)/shard_map/qhd,khd->hqk/dot_general | solution.py:207
  531.9 21.6 %multiply_convert_fusion = bf16[12,512,1024]{2,1,0:T(8,128)(2,1)} fusion(f32[12,512,1024]{2,1,0:T(8,128)} %get-tuple-element.86, f32[12,512,1024]{2,1,0:T(8,128)} %get-tuple-element.75, f32[12,512]{1,0:T(8,128)S(1)} %copy-done.52, f32[12,512]{1,0:T(8,128)S(1)} %copy-done.45), kind=kLoop, calls=%fused_computation.12 | loop fusion | flops 25165824 | bytes 62963712 | tf_op jit(solution)/shard_map/convert_element_type | solution.py:211
  588.0 13.5 %fusion.38 = bf16[1,3072,768]{2,1,0:T(8,128)(2,1)} fusion(bf16[16,1,80,768]{3,2,1,0:T(8,128)(2,1)S(1)} %copy-done.36, f32[16,80,3072]{2,1,0:T(8,128)} %copy-done.77), kind=kOutput, calls=%fused_computation.65 | convolution fusion | flops 6077546496 | bytes 22413312 | tf_op jit(solution)/shard_map/esrf,esrd->efd/dot_general | solution.py:162
  601.6 165.6 %all-reduce.7.cloned.1.call-done = (f32[768,768]{1,0:T(8,128)}, f32[768,768]{1,0:T(8,128)}, f32[768,768]{1,0:T(8,128)}, f32[768,768]{1,0:T(8,128)}) async-done(((f32[768,768]{1,0:T(8,128)}, f32[768,768]{1,0:T(8,128)}, f32[768,768]{1,0:T(8,128)}, f32[768,768]{1,0:T(8,128)}), (f32[768,768]{1,0:T(8,128)}, f32[768,768]{1,0:T(8,128)}, f32[768,768]{1,0:T(8,128)}, ...) | async-done | bytes 9437200 | tf_op jit(solution)/shard_map/psum | solution.py:255
  767.3 23.2 %copy.75 = bf16[12,512,1024]{1,0,2:T(8,128)(2,1)} copy(bf16[12,512,1024]{2,1,0:T(8,128)(2,1)} %multiply_convert_fusion.1) | data formatting | bytes 25165824 | tf_op jit(solution)/shard_map/convert_element_type | solution.py:211
  790.5 23.3 %copy.76 = bf16[12,512,1024]{1,0,2:T(8,128)(2,1)} copy(bf16[12,512,1024]{2,1,0:T(8,128)(2,1)} %multiply_convert_fusion) | data formatting | bytes 25165824 | tf_op jit(solution)/shard_map/convert_element_type | solution.py:211
  829.6 13.1 %fusion.86 = f32[32,12]{0,1:T(8,128)S(1)} fusion(bf16[12,512,1024]{1,0,2:T(8,128)(2,1)} %copy.75, s32[512,1024]{0,1:T(8,128)} %fusion.48), kind=kOutput, calls=%fused_computation.130 | convolution fusion | flops 419430400 | bytes 14681600 | tf_op jit(solution)/shard_map/qkb,hqk->bh/dot_general | solution.py:227
  842.8 13.9 %fusion.88 = f32[32,12]{0,1:T(8,128)S(1)} fusion(f32[32,12]{0,1:T(8,128)S(1)} %fusion.86, bf16[12,512,1024]{1,0,2:T(8,128)(2,1)} %copy.76, s32[512,1024]{0,1:T(8,128)S(1)} %copy-done.16), kind=kOutput, calls=%fused_computation.132 | convolution fusion | flops 419430784 | bytes 14683136 | tf_op jit(solution)/shard_map/qkb,hqk->bh/dot_general | solution.py:227
  856.7 60.6 %all-reduce = (f32[768]{0:T(1024)S(1)}, f32[32,12]{0,1:T(8,128)S(1)}, f32[768]{0:T(1024)S(1)}, f32[768,16]{0,1:T(8,128)S(1)}) all-reduce(f32[768]{0:T(1024)S(1)} %get-tuple-element.50, f32[32,12]{0,1:T(8,128)S(1)} %fusion.88, f32[768]{0:T(1024)S(1)} %copy-done.71, ...), channel_id=1, replica_groups=mesh['dp'=2,'expert'=16] {'expert'}, use_global_device_ids=true, to_apply=%region_18.19 | all-reduce | flops 14208 | bytes 113664 | tf_op jit(solution)/shard_map/psum | solution.py:255
  937.2 53.6 %all-reduce.9.cloned.1.call-done = (f32[768,768]{1,0:T(8,128)}, f32[768,768]{1,0:T(8,128)}, f32[768,768]{1,0:T(8,128)}, f32[768,768]{1,0:T(8,128)}) async-done(((f32[768,768]{1,0:T(8,128)}, f32[768,768]{1,0:T(8,128)}, f32[768,768]{1,0:T(8,128)}, f32[768,768]{1,0:T(8,128)}), (f32[768,768]{1,0:T(8,128)}, f32[768,768]{1,0:T(8,128)}, f32[768,768]{1,0:T(8,128)}, ...) | async-done | bytes 9437200 | tf_op jit(solution)/shard_map/psum | solution.py:268
  (248 shorter events, 300.5 us)
Async XLA Ops:
  8.0 22.6 %copy-start = (bf16[768,768]{1,0:T(8,128)(2,1)S(1)}, bf16[768,768]{1,0:T(8,128)(2,1)}, u32[]{:S(2)}) copy-start(bf16[768,768]{1,0:T(8,128)(2,1)} %param.19) | copy-start | bytes 3538948
  10.6 20.0 %copy-start.62 = (f32[768]{0:T(1024)}, f32[768]{0:T(1024)S(1)}, u32[]{:S(2)}) copy-start(f32[768]{0:T(1024)S(1)} %convert_element_type.295) | copy-start | bytes 9220
  27.4 141.6 %copy-start.17 = (bf16[512,768]{0,1:T(8,128)(2,1)}, bf16[512,768]{0,1:T(8,128)(2,1)S(1)}, u32[]{:S(2)}) copy-start(bf16[512,768]{0,1:T(8,128)(2,1)S(1)} %get-tuple-element.73) | copy-start | bytes 2359300
  30.7 138.3 %copy-start.4 = (bf16[1024,768]{0,1:T(8,128)(2,1)}, bf16[1024,768]{0,1:T(8,128)(2,1)S(1)}, u32[]{:S(2)}) copy-start(bf16[1024,768]{0,1:T(8,128)(2,1)S(1)} %convolution_convert_fusion.3) | copy-start | bytes 4718596
  214.0 13.9 %copy-start.11 = (bf16[1024,768]{0,1:T(8,128)(2,1)}, bf16[1024,768]{0,1:T(8,128)(2,1)S(1)}, u32[]{:S(2)}) copy-start(bf16[1024,768]{0,1:T(8,128)(2,1)S(1)} %multiply_convert_fusion.4) | copy-start | bytes 4718596
  217.5 46.6 %all-to-all-start = ((bf16[16,1,80,768]{3,2,1,0:T(8,128)(2,1)}), bf16[16,1,80,768]{3,2,1,0:T(8,128)(2,1)}, u32[]{:S(2)}, u32[]{:S(2)}) async-start(bf16[16,1,80,768]{3,2,1,0:T(8,128)(2,1)} %bitcast.181), calls=%async_computation | async-start | bytes 3932160 | tf_op jit(solution)/shard_map/all_to_all | solution.py:125
  228.2 189.3 %copy-start.37 = (f32[1024,16]{0,1:T(8,128)}, f32[1024,16]{0,1:T(8,128)S(1)}, u32[]{:S(2)}) copy-start(f32[1024,16]{0,1:T(8,128)S(1)} %get-tuple-element.81) | copy-start | bytes 196612
  228.2 189.3 %copy-start.55 = (f32[1024]{0:T(1024)}, f32[1024]{0:T(1024)S(1)}, u32[]{:S(2)}) copy-start(f32[1024]{0:T(1024)S(1)} %get-tuple-element.80) | copy-start | bytes 12292
  228.2 189.3 %copy-start.60 = (f32[1024]{0:T(1024)}, f32[1024]{0:T(1024)S(1)}, u32[]{:S(2)}) copy-start(f32[1024]{0:T(1024)S(1)} %fusion.101) | copy-start | bytes 12292
  264.1 49.5 %all-to-all-start.2 = ((bf16[16,1,80,768]{3,2,1,0:T(8,128)(2,1)}), bf16[16,1,80,768]{3,2,1,0:T(8,128)(2,1)S(1)}, u32[]{:S(2)}, u32[]{:S(2)}) async-start(bf16[16,1,80,768]{3,2,1,0:T(8,128)(2,1)} %bitcast.182), calls=%async_computation.2 | async-start | bytes 3932160 | tf_op jit(solution)/shard_map/all_to_all | solution.py:148
  313.6 28.4 %copy-start.35 = (bf16[16,1,80,768]{3,2,1,0:T(8,128)(2,1)}, bf16[16,1,80,768]{3,2,1,0:T(8,128)(2,1)S(1)}, u32[]{:S(2)}) copy-start(bf16[16,1,80,768]{3,2,1,0:T(8,128)(2,1)S(1)} %all-to-all-done.2) | copy-start | bytes 5898244
  313.6 49.8 %all-to-all-start.1 = ((bf16[1,16,80,768]{3,2,0,1:T(8,128)(2,1)}), bf16[1,16,80,768]{3,2,0,1:T(8,128)(2,1)}, u32[]{:S(2)}, u32[]{:S(2)}) async-start(bf16[1,16,80,768]{3,2,0,1:T(8,128)(2,1)} %convert_bitcast_fusion.1), calls=%async_computation.1 | async-start | bytes 3932160 | tf_op jit(solution)/shard_map/all_to_all | solution.py:133
  355.0 19.5 %copy-start.48 = (f32[12,512]{1,0:T(8,128)S(1)}, f32[12,512]{1,0:T(8,128)}, u32[]{:S(2)}) copy-start(f32[12,512]{1,0:T(8,128)} %get-tuple-element.76) | copy-start | bytes 73732
  355.0 19.5 %copy-start.54 = (f32[12,512]{1,0:T(8,128)S(1)}, f32[12,512]{1,0:T(8,128)}, u32[]{:S(2)}) copy-start(f32[12,512]{1,0:T(8,128)} %copy-done.53) | copy-start | bytes 73732
  355.0 20.8 %copy-start.27 = (bf16[1024,768]{0,1:T(8,128)(2,1)S(1)}, bf16[1024,768]{0,1:T(8,128)(2,1)}, u32[]{:S(2)}) copy-start(bf16[1024,768]{0,1:T(8,128)(2,1)} %copy.67) | copy-start | bytes 4718596
  363.5 49.6 %all-to-all-start.3 = ((bf16[1,16,80,768]{3,2,0,1:T(8,128)(2,1)}), bf16[1,16,80,768]{3,2,0,1:T(8,128)(2,1)}, u32[]{:S(2)}, u32[]{:S(2)}) async-start(bf16[1,16,80,768]{3,2,0,1:T(8,128)(2,1)} %convert_bitcast_fusion), calls=%async_computation.3 | async-start | bytes 3932160 | tf_op jit(solution)/shard_map/all_to_all | solution.py:158
  374.2 393.1 %all-reduce.7.cloned.1.call-start = ((), (), s32[]{:S(2)}) async-start(), calls=%async_computation.8 | async-start | bytes 18874368 | tf_op jit(solution)/shard_map/psum | solution.py:255
  381.7 35.9 %copy-start.68 = (f32[1024]{0:T(1024)}, f32[1024]{0:T(1024)S(1)}, u32[]{:S(2)}) copy-start(f32[1024]{0:T(1024)S(1)} %mul.288) | copy-start | bytes 12292
  448.3 21.7 %copy-start.5 = (bf16[1024,768]{0,1:T(8,128)(2,1)S(1)}, bf16[1024,768]{0,1:T(8,128)(2,1)}, u32[]{:S(2)}) copy-start(bf16[1024,768]{0,1:T(8,128)(2,1)} %copy-done.4) | copy-start | bytes 4718596
  575.2 353.1 %reduce-scatter.3.cloned.1.call-start = ((), (), s32[]{:S(2)}) async-start(), calls=%async_computation.6 | async-start | bytes 7077888 | tf_op jit(solution)/shard_map/reduce_scatter | solution.py:166
  585.9 346.8 %reduce-scatter.5.cloned.1.call-start = ((), (), s32[]{:S(2)}) async-start(), calls=%async_computation.7 | async-start | bytes 7077888 | tf_op jit(solution)/shard_map/reduce_scatter | solution.py:169
  601.6 389.3 %all-reduce.9.cloned.1.call-start = ((), (), s32[]{:S(2)}) async-start(), calls=%async_computation.9 | async-start | bytes 18874368 | tf_op jit(solution)/shard_map/psum | solution.py:268
  790.5 23.3 %copy-start.26 = (bf16[1024,768]{0,1:T(8,128)(2,1)S(1)}, bf16[1024,768]{0,1:T(8,128)(2,1)}, u32[]{:S(2)}) copy-start(bf16[1024,768]{0,1:T(8,128)(2,1)} %get-tuple-element.69) | copy-start | bytes 4718596
  842.7 13.9 %copy-start.71 = (f32[768]{0:T(1024)S(1)}, f32[768]{0:T(1024)}, u32[]{:S(2)}) copy-start(f32[768]{0:T(1024)} %get-tuple-element.48) | copy-start | bytes 9220
  (62 other events, 313.0 us)
Sparse Core Ops, SparseCore 0:
  575.3 191.9 all-reduce.6
Sparse Core Ops, SparseCore 1:
  586.0 65.9 reduce-scatter.2
  654.3 59.9 reduce-scatter.4
  767.4 223.4 all-reduce.8
